TPU v7x, 32 devices: a whole 2x2x4 slice. The times are simulated.
32 devices in a mesh: groups: 2 (over x), seq: 16 (over z, y, core).
Axes of the slice: x: 2, y: 2, z: 4, core: 2. Of those that a mesh axis runs over, the one named last changes fastest.
Arguments:
- queries: bfloat16 [32, 32, 1024], P('seq', 'groups'), parts along dimension 1, may hold values from -1100 to 1100
- keys: bfloat16 [32, 32, 128], P('seq', 'groups'), parts along dimension 1, may hold values from -4 to 4
- values: bfloat16 [32, 32, 128], P('seq', 'groups'), parts along dimension 1, may hold values from -6 to 6
- cache_keys: bfloat16 [32, 2048, 128], P(('groups', 'seq')), parts along dimension 0, may hold values from -4 to 4
- cache_values: bfloat16 [32, 2048, 128], P(('groups', 'seq')), parts along dimension 0, may hold values from -6 to 6
- cache_len: int32 [32, 16], P(None, 'groups'), parts along dimension 1, may hold values from 1 to 2048, as said below
- out_weight: bfloat16 [2048, 2048], P('seq'), may hold values from -0.5 to 0.5
- norm_gain: bfloat16 [2048], replicated, may hold values from 0.5 to 1.5
- expert_ids: int32 [32, 16, 8], P('seq', 'groups'), parts along dimension 1, may hold values from 0 to 31, all different within a row; in each aligned block of 16 rows (0 to 15, 16 to 31, ..., all dimensions but the last counted through in order) at most 5 rows name the same one
- route_weights: float32 [32, 16, 8], P('seq', 'groups'), parts along dimension 1, may hold values from 0.02 to 1
- w_gate: bfloat16 [32, 2048, 384], P('seq'), may hold values from -0.125 to 0.125
- w_up: bfloat16 [32, 2048, 384], P('seq'), may hold values from -0.125 to 0.125
- w_down: bfloat16 [32, 384, 2048], P('seq'), may hold values from -0.3125 to 0.3125
Outputs:
- projected: bfloat16 [32, 16, 2048], P('seq', 'groups'), parts along dimension 1
- moe_out: bfloat16 [32, 16, 2048], P('seq', 'groups'), parts along dimension 1
There are 2 independent parts, one for each index of `groups`. A program takes and returns all parts, laid end to end along the dimension named above; an argument that names none is the same for every part. Nothing has to cross between parts.
Inputs may be any that keep to these rules, and one draw needn't show every extreme that they name: `cache_len`: every new token sees at least one cached key; some token sees all 2048. `expert_ids`: rows are taken position-major over members; in each aligned block of 16 rows (the rows of one index of seq) no expert is named more than 5 times, a bound that some block reaches.
All inputs are finite; a program needn't handle non-finite values.
Results may differ from a plain program's by a relative error of at most 0.01.
Values may be sent and summed in bfloat16 or wider, within the bound.
No kernel may reach another device: no remote copies, remote signals or barrier semaphores. Data moves between devices by JAX's collectives and lax.ppermute only.
A program may use at most 64 MiB of HBM per device.

v0:
```python
import jax
import jax.numpy as jnp
from jax import lax
from jax.sharding import PartitionSpec as P

D = 2048
HD = 128
TOPK = 8
QH = 16
KVH = 2
CAP = 5


def attend(query_heads, key_rows, value_rows, lengths):
    new_count = query_heads.shape[0]
    cache_count = key_rows.shape[0] - new_count
    scores = jnp.einsum(
        "qhd,kd->hqk", query_heads, key_rows, preferred_element_type=jnp.float32
    ) * HD ** (-0.5)
    cached_ok = jnp.arange(cache_count, dtype=jnp.int32)[None, :] < lengths[:, None]
    causal_ok = (
        jnp.arange(new_count, dtype=jnp.int32)[None, :]
        <= jnp.arange(new_count, dtype=jnp.int32)[:, None]
    )
    visible = jnp.concatenate([cached_ok, causal_ok], axis=1)
    scores = jnp.where(visible[None], scores, -1e30)
    row_max = jnp.max(scores, axis=-1, keepdims=True)
    expo = jnp.exp(scores - row_max)
    row_sum = jnp.sum(expo, axis=-1, keepdims=True)
    weights = (expo / row_sum).astype(jnp.bfloat16)
    result = jnp.einsum("hqk,kd->qhd", weights, value_rows, preferred_element_type=jnp.float32)
    return result.astype(jnp.bfloat16).reshape(new_count, -1)


def body(
    queries,
    keys,
    values,
    cache_keys,
    cache_values,
    cache_len,
    out_weight,
    norm_gain,
    expert_ids,
    route_weights,
    w_gate,
    w_up,
    w_down,
):
    slot_count = lax.axis_size("seq")
    per_rows = queries.shape[0]
    members = slot_count // KVH
    group_q = QH // KVH
    new_count = per_rows * slot_count
    position_index = lax.axis_index("seq")
    member = position_index // KVH
    query_rows, key_new, value_new = (
        lax.all_to_all(queries, "seq", split_axis=1, concat_axis=0, tiled=True),
        lax.all_to_all(keys, "seq", split_axis=1, concat_axis=0, tiled=True),
        lax.all_to_all(values, "seq", split_axis=1, concat_axis=0, tiled=True),
    )
    key_rows = jnp.concatenate([cache_keys[0], key_new.reshape(new_count, HD)], axis=0)
    value_rows = jnp.concatenate([cache_values[0], value_new.reshape(new_count, HD)], axis=0)
    lengths = lax.dynamic_slice_in_dim(cache_len, member, 1, 1)[:, 0]
    attended = attend(query_rows.reshape(new_count, group_q, HD), key_rows, value_rows, lengths)
    returned_heads = lax.all_to_all(
        attended[:, None, :], "seq", split_axis=0, concat_axis=1, tiled=True
    )
    token_heads = returned_heads.reshape(per_rows * members, QH * HD)
    projected_f = jnp.dot(
        token_heads,
        lax.all_gather(out_weight, "seq", axis=0, tiled=True),
        preferred_element_type=jnp.float32,
    )
    projected_f = projected_f.reshape(per_rows, members, D)
    projected = projected_f.astype(jnp.bfloat16)
    token_count = per_rows * members
    flat_rows = projected.reshape(token_count, D).astype(jnp.float32)
    stats = jnp.mean(flat_rows * flat_rows, axis=-1, keepdims=True)
    normed = (flat_rows * lax.rsqrt(stats + 1e-06) * norm_gain.astype(jnp.float32)).astype(
        jnp.bfloat16
    )
    exp_dev = w_gate.shape[0]
    expert_count = exp_dev * slot_count
    chosen_ids = expert_ids.reshape(token_count * TOPK)
    onehot = (chosen_ids[:, None] == jnp.arange(expert_count, dtype=jnp.int32)[None, :]).astype(
        jnp.int32
    )
    slot_rank = jnp.sum((jnp.cumsum(onehot, axis=0) - onehot) * onehot, axis=1)
    owner = chosen_ids // exp_dev
    local_expert = chosen_ids % exp_dev
    slot_target = (local_expert * slot_count + owner) * CAP + slot_rank
    total_slots = exp_dev * slot_count * CAP
    token_of = jnp.arange(token_count * TOPK, dtype=jnp.int32) // TOPK
    source_row = jnp.full((total_slots,), -1, jnp.int32).at[slot_target].set(token_of)
    filled = source_row >= 0
    outgoing = jnp.where(
        filled[:, None], normed[jnp.maximum(source_row, 0)], jnp.zeros((), jnp.bfloat16)
    )
    outgoing = outgoing.reshape(exp_dev, slot_count, CAP, D)
    incoming = lax.all_to_all(outgoing, "seq", split_axis=1, concat_axis=1, tiled=True)
    row_block = incoming.reshape(exp_dev, slot_count * CAP, D)
    gate_out = jnp.einsum("ecd,edf->ecf", row_block, w_gate, preferred_element_type=jnp.float32)
    up_out = jnp.einsum("ecd,edf->ecf", row_block, w_up, preferred_element_type=jnp.float32)
    hidden_act = (jax.nn.silu(gate_out) * up_out).astype(jnp.bfloat16)
    expert_out = jnp.einsum(
        "ecf,efd->ecd", hidden_act, w_down, preferred_element_type=jnp.float32
    ).astype(jnp.bfloat16)
    expert_back = lax.all_to_all(
        expert_out.reshape(exp_dev, slot_count, CAP, D),
        "seq",
        split_axis=1,
        concat_axis=1,
        tiled=True,
    )
    picked = expert_back.reshape(total_slots, D)[slot_target].reshape(token_count, TOPK, D)
    raw_weights = route_weights.reshape(token_count, TOPK)
    norm_weights = raw_weights / jnp.sum(raw_weights, axis=1, keepdims=True)
    mixed = jnp.sum(norm_weights[:, :, None] * picked.astype(jnp.float32), axis=1)
    moe_out = mixed.astype(jnp.bfloat16).reshape(per_rows, members, D)
    return (projected, moe_out)


def solution(mesh):
    return jax.shard_map(
        body,
        mesh=mesh,
        in_specs=(
            P("seq", "groups", None),
            P("seq", "groups", None),
            P("seq", "groups", None),
            P(("groups", "seq"), None, None),
            P(("groups", "seq"), None, None),
            P(None, "groups"),
            P("seq", None),
            P(),
            P("seq", "groups", None),
            P("seq", "groups", None),
            P("seq", None, None),
            P("seq", None, None),
            P("seq", None, None),
        ),
        out_specs=(P("seq", "groups", None), P("seq", "groups", None)),
        check_vma=False,
    )
```

profile of v0, /device:TPU:0, one launch (start us, length us, event | category | flops | bytes accessed | tf_op | source)
XLA Modules:
  0.0 167.0 jit_solution(5124968312826070863)
XLA Ops:
  7.9 1.7 %copy.33 = bf16[2,16,1024]{2,0,1:T(2,128)(2,1)} copy(bf16[2,16,1024]{2,1,0:T(8,128)(2,1)} %param.13) | data formatting | bytes 131072 | tf_op args[0]
  9.7 7.4 %all-to-all-start.2 = ((bf16[2,16,1024]{2,0,1:T(2,128)(2,1)}), bf16[2,16,1024]{2,0,1:T(2,128)(2,1)S(1)}, u32[]{:S(2)}, u32[]{:S(2)}) async-start(bf16[2,16,1024]{2,0,1:T(2,128)(2,1)} %copy.33), calls=%async_computation.2 | async-start | bytes 131072 | tf_op jit(solution)/shard_map/all_to_all | solution.py:58
  17.1 0.8 eq.17
  17.9 0.8 reshape.224
  20.0 1.3 copy.32
  21.3 1.0 scatter_custom_fusion
  22.3 1.7 %all-to-all-done.2 = bf16[2,16,1024]{2,0,1:T(2,128)(2,1)S(1)} async-done(((bf16[2,16,1024]{2,0,1:T(2,128)(2,1)}), bf16[2,16,1024]{2,0,1:T(2,128)(2,1)S(1)}, u32[]{:S(2)}, u32[]{:S(2)}) %all-to-all-start.2) | async-done | bytes 65568 | tf_op jit(solution)/shard_map/all_to_all | solution.py:58
  24.0 4.3 %all-to-all-start.1 = ((bf16[2,16,128]{2,0,1:T(2,128)(2,1)}), bf16[2,16,128]{2,0,1:T(2,128)(2,1)S(1)}, u32[]{:S(2)}, u32[]{:S(2)}) async-start(bf16[2,16,128]{2,0,1:T(2,128)(2,1)} %copy.32), calls=%async_computation.1 | async-start | bytes 16384 | tf_op jit(solution)/shard_map/all_to_all | solution.py:59
  28.3 1.3 copy.31
  29.7 5.3 %all-to-all-done.1 = bf16[2,16,128]{2,0,1:T(2,128)(2,1)S(1)} async-done(((bf16[2,16,128]{2,0,1:T(2,128)(2,1)}), bf16[2,16,128]{2,0,1:T(2,128)(2,1)S(1)}, u32[]{:S(2)}, u32[]{:S(2)}) %all-to-all-start.1) | async-done | bytes 8224 | tf_op jit(solution)/shard_map/all_to_all | solution.py:59
  34.9 3.5 %all-to-all-start = ((bf16[2,16,128]{2,0,1:T(2,128)(2,1)}), bf16[2,16,128]{2,0,1:T(2,128)(2,1)S(1)}, u32[]{:S(2)}, u32[]{:S(2)}) async-start(bf16[2,16,128]{2,0,1:T(2,128)(2,1)} %copy.31), calls=%async_computation | async-start | bytes 16384 | tf_op jit(solution)/shard_map/all_to_all | solution.py:60
  38.4 3.4 %fusion.50 = (f32[8,32]{1,0:T(8,128)S(1)}, f32[8,32,2080]{2,1,0:T(8,128)}) fusion(pred[32,2080]{1,0:T(8,128)(4,1)S(1)} %pad_add_fusion, bf16[32,128]{1,0:T(8,128)(2,1)S(1)} %bitcast.89, bf16[2048,128]{1,0:T(8,128)(2,1)} %bitcast.91, bf16[32,8,128]{2,1,0:T(8,128)(2,1)S(1)} %reshape.222), kind=kOutput, calls=%fused_computation.81 | convolution fusion | flops 139511840 | bytes 2795520 | tf_op jit(solution)/shard_map/sub | solution.py:28
  41.8 2.9 %all-to-all-done = bf16[2,16,128]{2,0,1:T(2,128)(2,1)S(1)} async-done(((bf16[2,16,128]{2,0,1:T(2,128)(2,1)}), bf16[2,16,128]{2,0,1:T(2,128)(2,1)S(1)}, u32[]{:S(2)}, u32[]{:S(2)}) %all-to-all-start) | async-done | bytes 8224 | tf_op jit(solution)/shard_map/all_to_all | solution.py:60
  44.7 2.3 %fusion.11 = bf16[32,8,128]{2,0,1:T(8,128)(2,1)S(1)} fusion(f32[8,32,2080]{2,1,0:T(8,128)} %get-tuple-element.3, f32[8,32]{1,0:T(8,128)S(1)} %get-tuple-element.2, bf16[32,128]{1,0:T(8,128)(2,1)S(1)} %bitcast.90, bf16[2048,128]{1,0:T(8,128)(2,1)} %bitcast.92), kind=kOutput, calls=%fused_computation.17 | convolution fusion | flops 138477568 | bytes 2728960 | tf_op jit(solution)/shard_map/hqk,kd->qhd/dot_general | solution.py:31
  47.6 1.0 reduce.3
  49.3 3.5 %all-to-all-start.3 = ((bf16[16,2,1024]{2,1,0:T(2,128)(2,1)}), bf16[16,2,1024]{2,1,0:T(2,128)(2,1)S(1)}, u32[]{:S(2)}, u32[]{:S(2)}) async-start(bf16[16,2,1024]{2,1,0:T(2,128)(2,1)} %reshape.261), calls=%async_computation.3 | async-start | bytes 131072 | tf_op jit(solution)/shard_map/all_to_all | solution.py:66
  53.0 8.1 %all-to-all-done.3 = bf16[16,2,1024]{2,1,0:T(2,128)(2,1)S(1)} async-done(((bf16[16,2,1024]{2,1,0:T(2,128)(2,1)}), bf16[16,2,1024]{2,1,0:T(2,128)(2,1)S(1)}, u32[]{:S(2)}, u32[]{:S(2)}) %all-to-all-start.3) | async-done | bytes 65568 | tf_op jit(solution)/shard_map/all_to_all | solution.py:66
  61.6 26.4 %all-gather.2.cloned.1.call-done = bf16[2048,2048]{1,0:T(8,128)(2,1)} async-done(((bf16[128,2048]{1,0:T(8,128)(2,1)}), bf16[2048,2048]{1,0:T(8,128)(2,1)}) %all-gather.2.cloned.1.call-update) | async-done | bytes 8388624 | tf_op jit(solution)/shard_map/all_gather | solution.py:72
  88.0 4.7 %fusion.29 = (f32[2,8]{1,0:T(2,128)S(1)}, bf16[2,8,2048]{2,1,0:T(8,128)(2,1)S(1)}) fusion(bf16[2,8,2048]{2,1,0:T(8,128)(2,1)S(1)} %dot_general.22, bf16[2048,2048]{1,0:T(8,128)(2,1)} %all-gather.2.cloned.1.call-done), kind=kOutput, calls=%fused_computation.42 | convolution fusion | flops 134348784 | bytes 8519744 | tf_op jit(solution)/shard_map/dot_general | solution.py:70
  92.9 1.9 %gather_fusion = bf16[160,2048]{1,0:T(8,128)(2,1)} fusion(bf16[16,2048]{1,0:T(8,128)(2,1)S(1)} %fusion.28, s32[1024]{0:T(1024)S(1)} %pad_clamp_fusion.1), kind=kCustom, calls=%fused_computation | custom fusion | bytes 1311360 | tf_op jit(solution)/shard_map/gather | solution.py:98
  94.8 2.2 %gather.9 = bf16[2,16,5,2048]{3,2,1,0:T(8,128)(2,1)} reshape(bf16[160,2048]{1,0:T(8,128)(2,1)} %gather_fusion) | data formatting | bytes 1310720 | tf_op jit(solution)/shard_map/gather | solution.py:98
  97.0 1.5 broadcast_select_fusion
  99.3 21.4 %all_to_all.70 = bf16[2,16,5,2048]{3,0,2,1:T(2,128)(2,1)S(1)} all-to-all(bf16[2,16,5,2048]{3,0,2,1:T(2,128)(2,1)S(1)} %copy.40), channel_id=1, replica_groups=mesh['groups'=2,'seq'=16] {'seq'}, dimensions={1} | all-to-all | bytes 1310720 | tf_op jit(solution)/shard_map/all_to_all | solution.py:101
  120.7 0.9 copy-done.1
  122.3 4.3 %convolution_convert_fusion = bf16[2,80,2048]{2,1,0:T(8,128)(2,1)} fusion(bf16[2,384,2048]{2,1,0:T(8,128)(2,1)S(1)} %copy-done, bf16[2,2048,384]{2,1,0:T(8,128)(2,1)} %param.24, bf16[2,80,2048]{2,0,1:T(2,128)(2,1)} %bitcast.83, f32[2,80,384]{2,1,0:T(8,128)S(1)} %fusion.15), kind=kOutput, calls=%fused_computation.11 | convolution fusion | flops 504012800 | bytes 7847936 | tf_op jit(solution)/shard_map/ecf,efd->ecd/dot_general | solution.py:106
  126.6 2.6 %copy.43 = bf16[2,80,2048]{2,0,1:T(2,128)(2,1)} copy(bf16[2,80,2048]{2,1,0:T(8,128)(2,1)} %convolution_convert_fusion) | data formatting | bytes 1310720 | tf_op jit(solution)/shard_map/convert_element_type | solution.py:108
  129.2 4.3 %all-to-all-start.5 = ((bf16[2,16,5,2048]{3,0,2,1:T(2,128)(2,1)}), bf16[2,16,5,2048]{3,0,2,1:T(2,128)(2,1)}, u32[]{:S(2)}, u32[]{:S(2)}) async-start(bf16[2,16,5,2048]{3,0,2,1:T(2,128)(2,1)} %bitcast.84), calls=%async_computation.5 | async-start | bytes 1310720 | tf_op jit(solution)/shard_map/all_to_all | solution.py:109
  133.8 16.2 %all-to-all-done.5 = bf16[2,16,5,2048]{3,0,2,1:T(2,128)(2,1)} async-done(((bf16[2,16,5,2048]{3,0,2,1:T(2,128)(2,1)}), bf16[2,16,5,2048]{3,0,2,1:T(2,128)(2,1)}, u32[]{:S(2)}, u32[]{:S(2)}) %all-to-all-start.5) | async-done | bytes 655392 | tf_op jit(solution)/shard_map/all_to_all | solution.py:109
  150.1 2.4 %copy.44 = bf16[2,16,5,2048]{3,2,1,0:T(8,128)(2,1)} copy(bf16[2,16,5,2048]{3,0,2,1:T(2,128)(2,1)} %all-to-all-done.5) | data formatting | bytes 1310720 | tf_op jit(solution)/shard_map/all_to_all | solution.py:109
  152.4 2.2 %reshape.227 = bf16[160,2048]{1,0:T(8,128)(2,1)} reshape(bf16[2,16,5,2048]{3,2,1,0:T(8,128)(2,1)} %copy.44) | data formatting | bytes 1310720 | tf_op jit(solution)/shard_map/reshape | solution.py:116
  154.6 3.4 %gather_fusion.1 = bf16[128,2048]{1,0:T(8,128)(2,1)} fusion(bf16[160,2048]{1,0:T(8,128)(2,1)} %reshape.227, s32[1024]{0:T(1024)S(1)} %pad_clamp_fusion), kind=kCustom, calls=%fused_computation.1 | custom fusion | bytes 1049088 | tf_op jit(solution)/shard_map/gather | solution.py:116
  158.0 2.1 %fusion.12 = bf16[16,2048]{1,0:T(8,128)(2,1)} fusion(bf16[128,2048]{1,0:T(8,128)(2,1)} %gather_fusion.1, f32[16,8]{1,0:T(8,128)S(1)} %copy.39), kind=kLoop, calls=%fused_computation.19 | loop fusion | flops 753664 | bytes 590336 | tf_op jit(solution)/shard_map/reduce_sum | solution.py:119
  (48 shorter events, 5.9 us)
Async XLA Ops:
  7.2 115.2 %copy-start = (bf16[2,384,2048]{2,1,0:T(8,128)(2,1)S(1)}, bf16[2,384,2048]{2,1,0:T(8,128)(2,1)}, u32[]{:S(2)}) copy-start(bf16[2,384,2048]{2,1,0:T(8,128)(2,1)} %param.25) | copy-start | bytes 9437188
  7.2 80.9 %all-gather.2.cloned.1.call-start = ((), (), s32[]{:S(2)}) async-start(), calls=%async_computation.6 | async-start | bytes 8912896 | tf_op jit(solution)/shard_map/all_gather | solution.py:72
  9.7 14.3 %all-to-all-start.2 = ((bf16[2,16,1024]{2,0,1:T(2,128)(2,1)}), bf16[2,16,1024]{2,0,1:T(2,128)(2,1)S(1)}, u32[]{:S(2)}, u32[]{:S(2)}) async-start(bf16[2,16,1024]{2,0,1:T(2,128)(2,1)} %copy.33), calls=%async_computation.2 | async-start | bytes 131072 | tf_op jit(solution)/shard_map/all_to_all | solution.py:58
  24.0 10.9 %all-to-all-start.1 = ((bf16[2,16,128]{2,0,1:T(2,128)(2,1)}), bf16[2,16,128]{2,0,1:T(2,128)(2,1)S(1)}, u32[]{:S(2)}, u32[]{:S(2)}) async-start(bf16[2,16,128]{2,0,1:T(2,128)(2,1)} %copy.32), calls=%async_computation.1 | async-start | bytes 16384 | tf_op jit(solution)/shard_map/all_to_all | solution.py:59
  34.9 9.8 %all-to-all-start = ((bf16[2,16,128]{2,0,1:T(2,128)(2,1)}), bf16[2,16,128]{2,0,1:T(2,128)(2,1)S(1)}, u32[]{:S(2)}, u32[]{:S(2)}) async-start(bf16[2,16,128]{2,0,1:T(2,128)(2,1)} %copy.31), calls=%async_computation | async-start | bytes 16384 | tf_op jit(solution)/shard_map/all_to_all | solution.py:60
  44.7 8.1 %copy-start.5 = (bf16[2048]{0:T(1024)(128)(2,1)S(1)}, bf16[2048]{0:T(1024)(128)(2,1)}, u32[]{:S(2)}) copy-start(bf16[2048]{0:T(1024)(128)(2,1)} %param.20) | copy-start | bytes 12292
  49.3 11.8 %all-to-all-start.3 = ((bf16[16,2,1024]{2,1,0:T(2,128)(2,1)}), bf16[16,2,1024]{2,1,0:T(2,128)(2,1)S(1)}, u32[]{:S(2)}, u32[]{:S(2)}) async-start(bf16[16,2,1024]{2,1,0:T(2,128)(2,1)} %reshape.261), calls=%async_computation.3 | async-start | bytes 131072 | tf_op jit(solution)/shard_map/all_to_all | solution.py:66
  92.7 2.1 %copy-start.3 = (bf16[2,8,2048]{2,1,0:T(8,128)(2,1)}, bf16[2,8,2048]{2,1,0:T(8,128)(2,1)S(1)}, u32[]{:S(2)}) copy-start(bf16[2,8,2048]{2,1,0:T(8,128)(2,1)S(1)} %get-tuple-element.5) | copy-start | bytes 196612
  97.0 24.5 %copy-start.2 = (bf16[2,2048,384]{2,1,0:T(8,128)(2,1)S(1)}, bf16[2,2048,384]{2,1,0:T(8,128)(2,1)}, u32[]{:S(2)}) copy-start(bf16[2,2048,384]{2,1,0:T(8,128)(2,1)} %param.23) | copy-start | bytes 9437188
  120.7 0.9 copy-start.1
  126.6 6.9 %copy-start.4 = (f32[2,8,8]{2,1,0:T(8,128)S(1)}, f32[2,8,8]{2,1,0:T(8,128)}, u32[]{:S(2)}) copy-start(f32[2,8,8]{2,1,0:T(8,128)} %param.22) | copy-start | bytes 1540
  129.2 20.9 %all-to-all-start.5 = ((bf16[2,16,5,2048]{3,0,2,1:T(2,128)(2,1)}), bf16[2,16,5,2048]{3,0,2,1:T(2,128)(2,1)}, u32[]{:S(2)}, u32[]{:S(2)}) async-start(bf16[2,16,5,2048]{3,0,2,1:T(2,128)(2,1)} %bitcast.84), calls=%async_computation.5 | async-start | bytes 1310720 | tf_op jit(solution)/shard_map/all_to_all | solution.py:109
Sparse Core Ops, SparseCore 0:
  10.2 77.8 all-gather.1
where the time goes:
time: 168 us; the launch traced here: 167 us
  waiting for transfers between devices  61.4 us (37%)
  local copies, waits for them, and re-layouts  25.7 us (15%)
  starting transfers between devices  23 us (14%)
  blocking collectives  21.4 us (13%)
  matrix products  15.4 us (9%)
  between operations  14.3 us (9%)
  other arithmetic  5.82 us (3%)
    all_gather x1, waiting for transfers between devices, body(): lax.all_gather(out_weight, 'seq', axis=0, tiled=True)  26.4 us
    all_to_all x1, blocking collectives, body(): lax.all_to_all(outgoing, 'seq', split_axis=1, concat_axis=1, tiled=True)  21.4 us
    all_to_all x1, waiting for transfers between devices, body(): lax.all_to_all(expert_out.reshape(exp_dev, slot_count, CAP, D), 'seq', sp...  16.2 us
    all_to_all x1, waiting for transfers between devices, body(): lax.all_to_all(attended[:, None, :], 'seq', split_axis=0, concat_axis=1,...  8.13 us
    all_to_all x1, starting transfers between devices, body(): lax.all_to_all(queries, 'seq', split_axis=1, concat_axis=0, tiled=True)  7.41 us
    unnamed x17, local copies, waits for them, and re-layouts  5.94 us
    all_to_all x1, waiting for transfers between devices, body(): lax.all_to_all(keys, 'seq', split_axis=1, concat_axis=0, tiled=True)  5.26 us
    dot_general x1, matrix products, body(): jnp.dot(token_heads, lax.all_gather(out_weight, 'seq', axis=0, tiled=True...  4.66 us
  transfers between devices with their start and end apart: 6, of which 6 were waited for; matrix products, arithmetic and copies ran while one was open for 10% of the time, Pallas kernels for 0%

commit v1 on v0

--- a/solution.py
+++ b/solution.py
@@ -69,7 +69,9 @@
     token_heads = returned_heads.reshape(per_rows * members, QH * HD)
     projected_f = jnp.dot(
         token_heads,
-        lax.all_gather(out_weight, "seq", axis=0, tiled=True),
+        jnp.concatenate(
+            lax.all_to_all(jnp.stack([out_weight] * lax.axis_size("seq")), "seq", 0, 0), axis=0
+        ),
         preferred_element_type=jnp.float32,
     )
     projected_f = projected_f.reshape(per_rows, members, D)

time: 168 us -> 317 us (1.89)
  waiting for transfers between devices: 61.4 us -> 177 us
  blocking collectives: 21.4 us -> 64.3 us
  between operations: 14.3 us -> 0.93 us
  local copies, waits for them, and re-layouts: 25.7 us -> 29 us
    all_to_all x1, waiting for transfers between devices: 8.13 us -> 148 us  [body(): lax.all_to_all(jnp.stack([out_weight] * lax.axis_size('seq')), 'seq', 0, 0)]
    all_to_all x1, blocking collectives: 21.4 us -> 54.5 us  [body(): lax.all_to_all(outgoing, 'seq', split_axis=1, concat_axis=1, tiled=True)]
    all_gather x1 -> x0, waiting for transfers between devices: 26.4 us -> none  [body(): lax.all_gather(out_weight, 'seq', axis=0, tiled=True)]
    all_to_all x0 -> x1, blocking collectives: none -> 9.74 us  [body(): lax.all_to_all(attended[:, None, :], 'seq', split_axis=0, concat_axis=1,...]
    another operation x0 -> x1, local copies, waits for them, and re-layouts: none -> 5.32 us  [body(): jnp.stack([out_weight] * lax.axis_size('seq'))]
  transfers between devices with their start and end apart: 6 -> 5, of which waited for: 6 -> 5; matrix products, arithmetic and copies ran while one was open for 10% -> 3% of each run, Pallas kernels for 0% -> 0%
where the time goes in v1:
time: 317 us; the launch traced here: 316 us
  waiting for transfers between devices  177 us (56%)
  blocking collectives  64.3 us (20%)
  local copies, waits for them, and re-layouts  29 us (9%)
  starting transfers between devices  23.5 us (7%)
  matrix products  15.4 us (5%)
  other arithmetic  5.81 us (2%)
    all_to_all x1, waiting for transfers between devices, body(): lax.all_to_all(jnp.stack([out_weight] * lax.axis_size('seq')), 'seq', 0, 0)  148 us
    all_to_all x1, blocking collectives, body(): lax.all_to_all(outgoing, 'seq', split_axis=1, concat_axis=1, tiled=True)  54.5 us
    all_to_all x1, waiting for transfers between devices, body(): lax.all_to_all(expert_out.reshape(exp_dev, slot_count, CAP, D), 'seq', sp...  16.2 us
    all_to_all x1, blocking collectives, body(): lax.all_to_all(attended[:, None, :], 'seq', split_axis=0, concat_axis=1,...  9.74 us
    all_to_all x1, starting transfers between devices, body(): lax.all_to_all(queries, 'seq', split_axis=1, concat_axis=0, tiled=True)  7.41 us
  transfers between devices with their start and end apart: 5, of which 5 were waited for; matrix products, arithmetic and copies ran while one was open for 3% of the time, Pallas kernels for 0%

profile of v1, /device:TPU:0, one launch (start us, length us, event | category | flops | bytes accessed | tf_op | source)
XLA Modules:
  0.0 315.9 jit_solution(10542408048876071085)
XLA Ops:
  0.6 1.7 copy.33
  2.3 7.4 %all-to-all-start.2 = ((bf16[2,16,1024]{2,0,1:T(2,128)(2,1)}), bf16[2,16,1024]{2,0,1:T(2,128)(2,1)S(1)}, u32[]{:S(2)}, u32[]{:S(2)}) async-start(bf16[2,16,1024]{2,0,1:T(2,128)(2,1)} %copy.33), calls=%async_computation.2 | async-start | bytes 131072 | tf_op jit(solution)/shard_map/all_to_all | solution.py:58
  10.6 1.3 copy.32
  11.9 4.8 %all-to-all-done.2 = bf16[2,16,1024]{2,0,1:T(2,128)(2,1)S(1)} async-done(((bf16[2,16,1024]{2,0,1:T(2,128)(2,1)}), bf16[2,16,1024]{2,0,1:T(2,128)(2,1)S(1)}, u32[]{:S(2)}, u32[]{:S(2)}) %all-to-all-start.2) | async-done | bytes 65568 | tf_op jit(solution)/shard_map/all_to_all | solution.py:58
  16.7 3.5 %all-to-all-start.1 = ((bf16[2,16,128]{2,0,1:T(2,128)(2,1)}), bf16[2,16,128]{2,0,1:T(2,128)(2,1)S(1)}, u32[]{:S(2)}, u32[]{:S(2)}) async-start(bf16[2,16,128]{2,0,1:T(2,128)(2,1)} %copy.32), calls=%async_computation.1 | async-start | bytes 16384 | tf_op jit(solution)/shard_map/all_to_all | solution.py:59
  20.1 1.3 copy.31
  21.5 5.0 %all-to-all-done.1 = bf16[2,16,128]{2,0,1:T(2,128)(2,1)S(1)} async-done(((bf16[2,16,128]{2,0,1:T(2,128)(2,1)}), bf16[2,16,128]{2,0,1:T(2,128)(2,1)S(1)}, u32[]{:S(2)}, u32[]{:S(2)}) %all-to-all-start.1) | async-done | bytes 8224 | tf_op jit(solution)/shard_map/all_to_all | solution.py:59
  26.5 3.5 %all-to-all-start = ((bf16[2,16,128]{2,0,1:T(2,128)(2,1)}), bf16[2,16,128]{2,0,1:T(2,128)(2,1)S(1)}, u32[]{:S(2)}, u32[]{:S(2)}) async-start(bf16[2,16,128]{2,0,1:T(2,128)(2,1)} %copy.31), calls=%async_computation | async-start | bytes 16384 | tf_op jit(solution)/shard_map/all_to_all | solution.py:60
  29.9 3.4 %fusion.45 = (f32[8,32]{1,0:T(8,128)S(1)}, f32[8,32,2080]{2,1,0:T(8,128)}) fusion(pred[32,2080]{1,0:T(8,128)(4,1)S(1)} %pad_add_fusion, bf16[32,128]{1,0:T(8,128)(2,1)S(1)} %bitcast.86, bf16[2048,128]{1,0:T(8,128)(2,1)} %bitcast.88, bf16[32,8,128]{2,1,0:T(8,128)(2,1)S(1)} %reshape.227), kind=kOutput, calls=%fused_computation.79 | convolution fusion | flops 139511840 | bytes 2795520 | tf_op jit(solution)/shard_map/sub | solution.py:28
  33.3 2.9 all-to-all-done
  36.3 2.3 fusion.6
  39.2 1.0 reduce.3
  40.2 9.7 %all_to_all.75 = bf16[16,2,1024]{2,1,0:T(2,128)(2,1)S(1)} all-to-all(bf16[16,2,1024]{2,1,0:T(2,128)(2,1)S(1)} %reshape.267), channel_id=1, replica_groups=mesh['groups'=2,'seq'=16] {'seq'}, dimensions={0} | all-to-all | bytes 131072 | tf_op jit(solution)/shard_map/all_to_all | solution.py:66
  49.9 5.3 %stack.2 = bf16[16,128,2048]{2,1,0:T(8,128)(2,1)} broadcast(bf16[128,2048]{1,0:T(8,128)(2,1)} %param.19), dimensions={1,2} | broadcast | bytes 8912896 | tf_op jit(solution)/shard_map/stack | solution.py:73
  55.3 4.9 %all-to-all-start.4 = ((bf16[16,128,2048]{2,1,0:T(8,128)(2,1)}), bf16[16,128,2048]{2,1,0:T(8,128)(2,1)}, u32[]{:S(2)}, u32[]{:S(2)}) async-start(bf16[16,128,2048]{2,1,0:T(8,128)(2,1)} %stack.2), calls=%async_computation.4 | async-start | bytes 16777216 | tf_op jit(solution)/shard_map/all_to_all | solution.py:73
  60.8 1.0 scatter_custom_fusion
  62.5 148.2 %all-to-all-done.4 = bf16[16,128,2048]{2,1,0:T(8,128)(2,1)} async-done(((bf16[16,128,2048]{2,1,0:T(8,128)(2,1)}), bf16[16,128,2048]{2,1,0:T(8,128)(2,1)}, u32[]{:S(2)}, u32[]{:S(2)}) %all-to-all-start.4) | async-done | bytes 8388640 | tf_op jit(solution)/shard_map/all_to_all | solution.py:73
  210.6 4.7 %fusion.24 = (f32[2,8]{1,0:T(2,128)S(1)}, bf16[2,8,2048]{2,1,0:T(8,128)(2,1)S(1)}) fusion(bf16[2,8,2048]{2,1,0:T(8,128)(2,1)S(1)} %dot_general.22, bf16[2048,2048,1]{1,0,2:T(8,128)(2,1)} %bitcast.17), kind=kOutput, calls=%fused_computation.40 | convolution fusion | flops 134348784 | bytes 8519744 | tf_op jit(solution)/shard_map/dot_general | solution.py:70
  215.5 1.9 gather_fusion
  217.4 2.2 gather.9
  219.6 1.5 broadcast_select_fusion
  221.9 54.5 %all_to_all.76 = bf16[2,16,5,2048]{3,0,2,1:T(2,128)(2,1)S(1)} all-to-all(bf16[2,16,5,2048]{3,0,2,1:T(2,128)(2,1)S(1)} %copy.40), channel_id=1, replica_groups=mesh['groups'=2,'seq'=16] {'seq'}, dimensions={1} | all-to-all | bytes 1310720 | tf_op jit(solution)/shard_map/all_to_all | solution.py:103
  276.5 0.9 copy-done.1
  277.3 0.8 fusion.10
  278.1 4.2 %convolution_convert_fusion = bf16[2,80,2048]{2,1,0:T(8,128)(2,1)} fusion(bf16[2,384,2048]{2,1,0:T(8,128)(2,1)S(1)} %copy-done, bf16[2,2048,384]{2,1,0:T(8,128)(2,1)} %param.24, bf16[2,80,2048]{2,0,1:T(2,128)(2,1)} %bitcast.80, f32[2,80,384]{2,1,0:T(8,128)S(1)} %fusion.10), kind=kOutput, calls=%fused_computation.9 | convolution fusion | flops 504012800 | bytes 7847936 | tf_op jit(solution)/shard_map/ecf,efd->ecd/dot_general | solution.py:108
  282.4 2.6 copy.43
  285.0 4.3 %all-to-all-start.6 = ((bf16[2,16,5,2048]{3,0,2,1:T(2,128)(2,1)}), bf16[2,16,5,2048]{3,0,2,1:T(2,128)(2,1)}, u32[]{:S(2)}, u32[]{:S(2)}) async-start(bf16[2,16,5,2048]{3,0,2,1:T(2,128)(2,1)} %bitcast.81), calls=%async_computation.6 | async-start | bytes 1310720 | tf_op jit(solution)/shard_map/all_to_all | solution.py:111
  289.6 16.2 %all-to-all-done.6 = bf16[2,16,5,2048]{3,0,2,1:T(2,128)(2,1)} async-done(((bf16[2,16,5,2048]{3,0,2,1:T(2,128)(2,1)}), bf16[2,16,5,2048]{3,0,2,1:T(2,128)(2,1)}, u32[]{:S(2)}, u32[]{:S(2)}) %all-to-all-start.6) | async-done | bytes 655392 | tf_op jit(solution)/shard_map/all_to_all | solution.py:111
  305.8 2.4 copy.44
  308.2 2.2 reshape.233
  310.4 3.4 %gather_fusion.1 = bf16[128,2048]{1,0:T(8,128)(2,1)} fusion(bf16[160,2048]{1,0:T(8,128)(2,1)} %reshape.233, s32[1024]{0:T(1024)S(1)} %pad_clamp_fusion), kind=kCustom, calls=%fused_computation.1 | custom fusion | bytes 1049088 | tf_op jit(solution)/shard_map/gather | solution.py:118
  313.8 2.1 fusion.7
  (49 shorter events, 4.0 us)
Async XLA Ops:
  0.6 277.5 %copy-start = (bf16[2,384,2048]{2,1,0:T(8,128)(2,1)S(1)}, bf16[2,384,2048]{2,1,0:T(8,128)(2,1)}, u32[]{:S(2)}) copy-start(bf16[2,384,2048]{2,1,0:T(8,128)(2,1)} %param.25) | copy-start | bytes 9437188
  2.3 14.3 %all-to-all-start.2 = ((bf16[2,16,1024]{2,0,1:T(2,128)(2,1)}), bf16[2,16,1024]{2,0,1:T(2,128)(2,1)S(1)}, u32[]{:S(2)}, u32[]{:S(2)}) async-start(bf16[2,16,1024]{2,0,1:T(2,128)(2,1)} %copy.33), calls=%async_computation.2 | async-start | bytes 131072 | tf_op jit(solution)/shard_map/all_to_all | solution.py:58
  16.7 9.8 %all-to-all-start.1 = ((bf16[2,16,128]{2,0,1:T(2,128)(2,1)}), bf16[2,16,128]{2,0,1:T(2,128)(2,1)S(1)}, u32[]{:S(2)}, u32[]{:S(2)}) async-start(bf16[2,16,128]{2,0,1:T(2,128)(2,1)} %copy.32), calls=%async_computation.1 | async-start | bytes 16384 | tf_op jit(solution)/shard_map/all_to_all | solution.py:59
  26.5 9.8 %all-to-all-start = ((bf16[2,16,128]{2,0,1:T(2,128)(2,1)}), bf16[2,16,128]{2,0,1:T(2,128)(2,1)S(1)}, u32[]{:S(2)}, u32[]{:S(2)}) async-start(bf16[2,16,128]{2,0,1:T(2,128)(2,1)} %copy.31), calls=%async_computation | async-start | bytes 16384 | tf_op jit(solution)/shard_map/all_to_all | solution.py:60
  55.3 4.9 %copy-start.5 = (s32[2,8,8]{2,1,0:T(8,128)S(1)}, s32[2,8,8]{2,1,0:T(8,128)}, u32[]{:S(2)}) copy-start(s32[2,8,8]{2,1,0:T(8,128)} %param.21) | copy-start | bytes 1540
  55.3 5.1 %copy-start.6 = (bf16[2048]{0:T(1024)(128)(2,1)S(1)}, bf16[2048]{0:T(1024)(128)(2,1)}, u32[]{:S(2)}) copy-start(bf16[2048]{0:T(1024)(128)(2,1)} %param.20) | copy-start | bytes 12292
  55.3 155.4 %all-to-all-start.4 = ((bf16[16,128,2048]{2,1,0:T(8,128)(2,1)}), bf16[16,128,2048]{2,1,0:T(8,128)(2,1)}, u32[]{:S(2)}, u32[]{:S(2)}) async-start(bf16[16,128,2048]{2,1,0:T(8,128)(2,1)} %stack.2), calls=%async_computation.4 | async-start | bytes 16777216 | tf_op jit(solution)/shard_map/all_to_all | solution.py:73
  215.3 2.1 copy-start.3
  219.6 57.7 %copy-start.2 = (bf16[2,2048,384]{2,1,0:T(8,128)(2,1)S(1)}, bf16[2,2048,384]{2,1,0:T(8,128)(2,1)}, u32[]{:S(2)}) copy-start(bf16[2,2048,384]{2,1,0:T(8,128)(2,1)} %param.23) | copy-start | bytes 9437188
  276.5 0.9 copy-start.1
  282.4 6.9 %copy-start.4 = (f32[2,8,8]{2,1,0:T(8,128)S(1)}, f32[2,8,8]{2,1,0:T(8,128)}, u32[]{:S(2)}) copy-start(f32[2,8,8]{2,1,0:T(8,128)} %param.22) | copy-start | bytes 1540
  285.0 20.9 %all-to-all-start.6 = ((bf16[2,16,5,2048]{3,0,2,1:T(2,128)(2,1)}), bf16[2,16,5,2048]{3,0,2,1:T(2,128)(2,1)}, u32[]{:S(2)}, u32[]{:S(2)}) async-start(bf16[2,16,5,2048]{3,0,2,1:T(2,128)(2,1)} %bitcast.81), calls=%async_computation.6 | async-start | bytes 1310720 | tf_op jit(solution)/shard_map/all_to_all | solution.py:111
